TPU v7x, 256 devices: a whole 4x4x8 slice. The times are simulated.
256 devices in a mesh: lon: 32 (over x, z_lo, core), lat: 8 (over y, z_hi).
Axes of the slice: x: 4, y: 4, z: 8 (z_hi: 2, z_lo: 4; z = z_hi * 4 + z_lo), core: 2. Of those that a mesh axis runs over, the one named last changes fastest.
Arguments:
- state: float32 [3, 256, 64, 8192], P(None, None, 'lat', 'lon'), may hold values from -6 to 6
- bathymetry: float32 [64, 8192], P('lat', 'lon'), may hold values from 0.5 to 2
- obs_index: int32 [8, 32, 256], P('lat', 'lon'), may hold values from 0 to 2047
- obs_count: int32 [8, 32], P('lat', 'lon'), may hold values from 85 to 256, as said below
- obs_value: float32 [8, 32, 256], P('lat', 'lon'), may hold values from -6 to 6
- obs_sd: float32 [8, 32, 256], P('lat', 'lon'), may hold values from 0.5 to 2
Outputs:
- analysis: float32 [3, 256, 64, 8192], P(None, None, 'lat', 'lon')
Inputs may be any that keep to these rules, and one draw needn't show every extreme that they name: `obs_count`: at least 85 slots of every tile are used; at least one tile uses all 256. `obs_index`: several slots may name the same cell.
All inputs are finite; a program needn't handle non-finite values.
Results may differ from a plain program's by a relative error of at most 0.000051.
Values sent between devices are 32-bit elements; how exact they have to be, the bound alone decides.
No kernel may reach another device: no remote copies, remote signals or barrier semaphores. Data moves between devices by JAX's collectives and lax.ppermute only.
A program may use at most 128 MiB of HBM per device.

v0:
```python
import math
import jax
import jax.numpy as jnp
from jax import lax
from jax.sharding import PartitionSpec as P


def with_halo(value, sides, width, wrap):
    for axis, dim in sides:
        count, length = (lax.axis_size(axis), value.shape[dim])
        up = [(i, (i + 1) % count) for i in range(count if wrap else count - 1)]
        down = [(j, i) for i, j in up]
        last = lax.slice_in_dim(value, length - width, length, axis=dim)
        first = lax.slice_in_dim(value, 0, width, axis=dim)
        before = lax.ppermute(last, axis, up)
        after = lax.ppermute(first, axis, down)
        value = jnp.concatenate([before, value, after], axis=dim)
    return value


def coriolis(rows, total):
    return jnp.sin(math.pi / 3.0 * ((rows.astype(jnp.float32) + 0.5) / total - 0.5))[:, None]


def extend(field, width):
    wide = with_halo(field, (("lat", 2),), width, False)
    return with_halo(wide, (("lon", 3),), width, True)


def new_height(height, flux, keep):
    div = (
        flux[0][:, 1:-1, 2:] - flux[0][:, 1:-1, :-2] + flux[1][:, 2:, 1:-1] - flux[1][:, :-2, 1:-1]
    )
    return (height - 0.25 * div) * keep


def new_wind(east, north, height, fcor, keep):
    grad_x = height[:, 1:-1, 2:] - height[:, 1:-1, :-2]
    grad_y = height[:, 2:, 1:-1] - height[:, :-2, 1:-1]
    east_new = (east + 0.5 * (fcor * north - 0.5 * grad_x)) * keep
    north_new = (north - 0.5 * (fcor * east + 0.5 * grad_y)) * keep
    return (east_new, north_new)


def shards(state, bathymetry, obs_index, obs_count, obs_value, obs_sd):
    members, nrows, ncols = (state.shape[1], state.shape[2], state.shape[3])
    total_rows = nrows * lax.axis_size("lat")
    base = lax.axis_index("lat") * nrows
    fcor = coriolis(base + jnp.arange(nrows), total_rows)
    height, east, north = (state[0], state[1], state[2])
    for step in range(2):
        flux = extend(jnp.stack([bathymetry * east, bathymetry * north]), 1)
        height = new_height(height, flux, 1.0)
        tall = extend(height[None], 1)[0]
        east, north = new_wind(east, north, tall, fcor, 1.0)
    slots = obs_index.shape[2]
    flat_height = height.reshape(members, nrows * ncols)
    hx = jnp.take(flat_height, obs_index.reshape(-1), axis=1)
    valid = (jnp.arange(slots) < obs_count.reshape(())).astype(jnp.float32)
    sigma = obs_sd.reshape(-1) * (
        math.sqrt(slots * lax.axis_size("lat") * lax.axis_size("lon")) / 16.0
    )
    hmean = jnp.mean(hx, axis=0)
    anomal = (hx - hmean) / (math.sqrt(members - 1) * sigma) * valid
    innov = (obs_value.reshape(-1) - hmean) / sigma * valid
    gram = jnp.dot(anomal, anomal.T, precision=lax.Precision.HIGHEST)
    proj = jnp.dot(anomal, innov, precision=lax.Precision.HIGHEST)
    gram, proj = lax.psum((gram, proj), ("lon", "lat"))
    eye = jnp.eye(members, dtype=jnp.float32)
    lower = jnp.linalg.cholesky(gram + eye)
    inv_lower = jax.scipy.linalg.solve_triangular(lower, eye, lower=True)
    weights = jax.scipy.linalg.cho_solve((lower, True), proj)
    transform = inv_lower.T + weights[:, None] / math.sqrt(members - 1)
    fields = jnp.stack([height, east, north])
    center = jnp.mean(fields, axis=1, keepdims=True)
    mixed = jnp.einsum("nm,cnab->cmab", transform, fields - center, precision=lax.Precision.HIGHEST)
    return center + mixed


def solution(mesh):
    return jax.shard_map(
        shards,
        mesh=mesh,
        in_specs=(
            P(None, None, "lat", "lon"),
            P("lat", "lon"),
            P("lat", "lon", None),
            P("lat", "lon"),
            P("lat", "lon", None),
            P("lat", "lon", None),
        ),
        out_specs=P(None, None, "lat", "lon"),
        check_vma=False,
    )
```

profile of v0, /device:TPU:8, one launch (start us, length us, event | category | flops | bytes accessed | tf_op | source)
XLA Modules:
  0.0 587.8 jit_solution(7116847816058828899)
XLA Ops:
  27.2 9.1 %collective-permute-start = (f32[2,256,1,256]{1,0,3,2:T(2,128)S(1)}, f32[2,256,1,256]{1,0,3,2:T(2,128)S(1)}, u32[]{:S(2)}, u32[]{:S(2)}) collective-permute-start(f32[2,256,1,256]{1,0,3,2:T(2,128)S(1)} %get-tuple-element.44), channel_id=1, source_target_pairs={{0,1},{1,2},{2,3},{3,4},{4,5},{5,6},{6,7},{8,9},{9,10},{10,11},{11... | collective-permute-start | bytes 1572872 | tf_op jit(solution)/shard_map/ppermute | solution.py:15
  38.3 12.9 %collective-permute-done = f32[2,256,1,256]{1,0,3,2:T(2,128)S(1)} collective-permute-done((f32[2,256,1,256]{1,0,3,2:T(2,128)S(1)}, f32[2,256,1,256]{1,0,3,2:T(2,128)S(1)}, u32[]{:S(2)}, u32[]{:S(2)}) %collective-permute-start) | collective-permute-done | bytes 524320 | tf_op jit(solution)/shard_map/ppermute | solution.py:15
  51.2 30.3 %collective-permute-done.1 = f32[2,256,1,256]{1,0,3,2:T(2,128)S(1)} collective-permute-done((f32[2,256,1,256]{1,0,3,2:T(2,128)S(1)}, f32[2,256,1,256]{1,0,3,2:T(2,128)S(1)}, u32[]{:S(2)}, u32[]{:S(2)}) %collective-permute-start.1) | collective-permute-done | bytes 524320 | tf_op jit(solution)/shard_map/ppermute | solution.py:16
  81.6 5.9 %collective-permute-start.3 = (f32[2,256,10,1]{1,0,3,2:T(2,128)S(1)}, f32[2,256,10,1]{1,0,3,2:T(2,128)S(1)}, u32[]{:S(2)}, u32[]{:S(2)}) collective-permute-start(f32[2,256,10,1]{1,0,3,2:T(2,128)S(1)} %get-tuple-element.41), channel_id=1, source_target_pairs={{8,0},{16,8},{24,16},{32,24},{40,32},{48,40},{56,48},{64,56},{72,6... | collective-permute-start | bytes 61448 | tf_op jit(solution)/shard_map/ppermute | solution.py:16
  90.4 9.7 %pad_maximum_fusion.2 = f32[2,256,10,258]{1,0,3,2:T(2,128)} fusion(f32[2,256,10,1]{1,0,3,2:T(2,128)S(1)} %collective-permute-done.3, f32[2,256,1,256]{1,0,3,2:T(2,128)S(1)} %collective-permute-done.1, f32[1,256,8,256]{1,0,3,2:T(1,128)} %copy-done, f32[1,256,8,256]{1,0,3,2:T(1,128)S(1)} %copy.43, f32[2,256,1,256]{1,0,3,2:T(2,128)S(1)} %collective-permute-done, ...), kind=kLoop, calls=%fused_computation.8 | loop fusion | flops 6604800 | bytes 10567680 | tf_op jit(solution)/shard_map/concatenate | solution.py:17
  100.1 10.4 %fusion.63 = (f32[1,256,10,258]{1,0,3,2:T(1,128)S(1)}, f32[1,256,10,258]{1,0,3,2:T(1,128)}) fusion(f32[2,256,10,258]{1,0,3,2:T(2,128)} %pad_maximum_fusion.2), kind=kLoop, calls=%fused_computation.141 | loop fusion | bytes 10567680 | tf_op jit(solution)/shard_map/slice | solution.py:32
  113.6 9.3 %collective-permute-start.4 = (f32[1,256,1,256]{1,3,2,0:T(8,128)S(1)}, f32[1,256,1,256]{1,3,2,0:T(8,128)S(1)}, u32[]{:S(2)}, u32[]{:S(2)}) collective-permute-start(f32[1,256,1,256]{1,3,2,0:T(8,128)S(1)} %get-tuple-element.52), channel_id=1, source_target_pairs={{0,1},{1,2},{2,3},{3,4},{4,5},{5,6},{6,7},{8,9},{9,10},{10,11},{11... | collective-permute-start | bytes 786440 | tf_op jit(solution)/shard_map/ppermute | solution.py:15
  125.0 10.7 %collective-permute-done.4 = f32[1,256,1,256]{1,3,2,0:T(8,128)S(1)} collective-permute-done((f32[1,256,1,256]{1,3,2,0:T(8,128)S(1)}, f32[1,256,1,256]{1,3,2,0:T(8,128)S(1)}, u32[]{:S(2)}, u32[]{:S(2)}) %collective-permute-start.4) | collective-permute-done | bytes 262176 | tf_op jit(solution)/shard_map/ppermute | solution.py:15
  135.7 6.7 %collective-permute-done.5 = f32[1,256,1,256]{1,3,2,0:T(8,128)S(1)} collective-permute-done((f32[1,256,1,256]{1,3,2,0:T(8,128)S(1)}, f32[1,256,1,256]{1,3,2,0:T(8,128)S(1)}, u32[]{:S(2)}, u32[]{:S(2)}) %collective-permute-start.5) | collective-permute-done | bytes 262176 | tf_op jit(solution)/shard_map/ppermute | solution.py:16
  144.1 5.8 collective-permute-start.7
  164.1 6.4 %collective-permute-start.8 = (f32[2,256,1,256]{1,3,2,0:T(8,128)S(1)}, f32[2,256,1,256]{1,3,2,0:T(8,128)S(1)}, u32[]{:S(2)}, u32[]{:S(2)}) collective-permute-start(f32[2,256,1,256]{1,3,2,0:T(8,128)S(1)} %get-tuple-element.42), channel_id=1, source_target_pairs={{0,1},{1,2},{2,3},{3,4},{4,5},{5,6},{6,7},{8,9},{9,10},{10,11},{11... | collective-permute-start | bytes 1572872 | tf_op jit(solution)/shard_map/ppermute | solution.py:15
  176.5 17.5 %collective-permute-done.8 = f32[2,256,1,256]{1,3,2,0:T(8,128)S(1)} collective-permute-done((f32[2,256,1,256]{1,3,2,0:T(8,128)S(1)}, f32[2,256,1,256]{1,3,2,0:T(8,128)S(1)}, u32[]{:S(2)}, u32[]{:S(2)}) %collective-permute-start.8) | collective-permute-done | bytes 524320 | tf_op jit(solution)/shard_map/ppermute | solution.py:15
  194.2 7.5 %collective-permute-start.11 = (f32[2,256,10,1]{1,0,3,2:T(2,128)S(1)}, f32[2,256,10,1]{1,0,3,2:T(2,128)S(1)}, u32[]{:S(2)}, u32[]{:S(2)}) collective-permute-start(f32[2,256,10,1]{1,0,3,2:T(2,128)S(1)} %copy.50), channel_id=1, source_target_pairs={{8,0},{16,8},{24,16},{32,24},{40,32},{48,40},{56,48},{64,56},{72,6... | collective-permute-start | bytes 61448 | tf_op jit(solution)/shard_map/ppermute | solution.py:16
  202.1 13.5 %collective-permute-done.10 = f32[2,256,10,1]{1,0,3,2:T(2,128)S(1)} collective-permute-done((f32[2,256,10,1]{1,0,3,2:T(2,128)S(1)}, f32[2,256,10,1]{1,0,3,2:T(2,128)S(1)}, u32[]{:S(2)}, u32[]{:S(2)}) %collective-permute-start.10) | collective-permute-done | bytes 20512 | tf_op jit(solution)/shard_map/ppermute | solution.py:15
  223.9 7.3 %collective-permute-start.12 = (f32[1,256,1,256]{1,3,2,0:T(8,128)}, f32[1,256,1,256]{1,3,2,0:T(8,128)S(1)}, u32[]{:S(2)}, u32[]{:S(2)}) collective-permute-start(f32[1,256,1,256]{1,3,2,0:T(8,128)} %get-tuple-element.50), channel_id=1, source_target_pairs={{0,1},{1,2},{2,3},{3,4},{4,5},{5,6},{6,7},{8,9},{9,10},{10,11},{11... | collective-permute-start | bytes 786440 | tf_op jit(solution)/shard_map/ppermute | solution.py:15
  231.2 5.8 collective-permute-start.13
  237.2 79.0 %psum.15 = f32[256]{0:T(256)S(1)} all-reduce(f32[256]{0:T(256)S(1)} %bitcast.156), channel_id=1, replica_groups=mesh['lon'=32,'lat'=8] {'lon','lat'}, use_global_device_ids=true, to_apply=%region_7.8 | all-reduce | flops 256 | bytes 2048 | tf_op jit(solution)/shard_map/psum | solution.py:68
  316.2 167.4 %all-reduce.3.cloned.1.call-done = f32[256,256]{0,1:T(8,128)} async-done(((f32[256,256]{0,1:T(8,128)}), f32[256,256]{0,1:T(8,128)}) %all-reduce.3.cloned.1.call-update) | async-done | bytes 262160 | tf_op jit(solution)/shard_map/psum | solution.py:68
  485.8 11.7 %cholesky.49 = f32[128,128]{1,0:T(8,128)S(1)} custom-call(f32[128,128]{1,0:T(8,128)S(1)} %cholesky.115), custom_call_target="Cholesky" | custom-call | tf_op jit(solution)/shard_map/jit(cholesky)/cholesky | solution.py:70
  497.5 9.8 %custom-call.21 = f32[1,128,128]{1,2,0:T(8,128)S(1)} custom-call(f32[1,128,128]{2,1,0:T(8,128)S(1)} %get-tuple-element.57), custom_call_target="InvertDiagBlocksLowerTriangular" | custom-call | tf_op jit(solution)/shard_map/jit(cholesky)/cholesky | solution.py:70
  507.8 11.7 %cholesky.103 = f32[128,128]{1,0:T(8,128)S(1)} custom-call(f32[128,128]{1,0:T(8,128)S(1)} %convolution_subtract_fusion.1), custom_call_target="Cholesky" | custom-call | tf_op jit(solution)/shard_map/jit(cholesky)/cholesky | solution.py:70
  527.5 20.6 %custom-call.22 = f32[2,128,128]{1,2,0:T(8,128)S(1)} custom-call(f32[2,128,128]{2,1,0:T(8,128)} %get-tuple-element.12), custom_call_target="InvertDiagBlocksLowerTriangular" | custom-call | tf_op jit(solution)/shard_map/jit(_solve_triangular)/triangular_solve | solution.py:71
  567.0 7.1 %add_bitcast_fusion = f32[3,256,8,256]{1,3,2,0:T(8,128)} fusion(f32[3,8,256]{2,1,0:T(8,128)S(1)} %broadcast_multiply_fusion.2, f32[1,256,8,256]{1,3,2,0:T(8,128)S(1)} %get-tuple-element.30, f32[1,256,8,256]{1,3,2,0:T(8,128)S(1)} %get-tuple-element.29, f32[1,256,8,256]{1,3,2,0:T(8,128)S(1)} %bitcast.145, f32[128,256]{1,0:T(8,128)S(1)} %fusion.48, ...), kind=kOutput, calls=%fused_computation.4 | convolution fusion | flops 4838260736 | bytes 12870656 | tf_op jit(solution)/shard_map/nm,cnab->cmab/dot_general | solution.py:76
  574.0 6.6 %copy.59 = f32[3,256,8,256]{3,2,1,0:T(8,128)} copy(f32[3,256,8,256]{1,3,2,0:T(8,128)} %add_bitcast_fusion) | data formatting | bytes 12582912 | tf_op jit(solution)/shard_map/add | solution.py:77
  (148 shorter events, 93.8 us)
Async XLA Ops:
  6.5 477.1 %all-reduce.3.cloned.1.call-start = ((), (), s32[]{:S(2)}) async-start(), calls=%async_computation | async-start | bytes 524288 | tf_op jit(solution)/shard_map/psum | solution.py:68
  26.3 55.2 %copy-start = (f32[1,256,8,256]{1,0,3,2:T(1,128)}, f32[1,256,8,256]{1,0,3,2:T(1,128)S(1)}, u32[]{:S(2)}) copy-start(f32[1,256,8,256]{1,0,3,2:T(1,128)S(1)} %broadcast_multiply_fusion) | copy-start | bytes 6291460
  27.2 24.0 %collective-permute-start = (f32[2,256,1,256]{1,0,3,2:T(2,128)S(1)}, f32[2,256,1,256]{1,0,3,2:T(2,128)S(1)}, u32[]{:S(2)}, u32[]{:S(2)}) collective-permute-start(f32[2,256,1,256]{1,0,3,2:T(2,128)S(1)} %get-tuple-element.44), channel_id=1, source_target_pairs={{0,1},{1,2},{2,3},{3,4},{4,5},{5,6},{6,7},{8,9},{9,10},{10,11},{11... | collective-permute-start | bytes 1572872 | tf_op jit(solution)/shard_map/ppermute | solution.py:15
  36.3 45.1 %collective-permute-start.1 = (f32[2,256,1,256]{1,0,3,2:T(2,128)S(1)}, f32[2,256,1,256]{1,0,3,2:T(2,128)S(1)}, u32[]{:S(2)}, u32[]{:S(2)}) collective-permute-start(f32[2,256,1,256]{1,0,3,2:T(2,128)S(1)} %get-tuple-element.45), channel_id=1, source_target_pairs={{1,0},{2,1},{3,2},{4,3},{5,4},{6,5},{7,6},{9,8},{10,9},{11,10},{12... | collective-permute-start | bytes 1572872 | tf_op jit(solution)/shard_map/ppermute | solution.py:16
  81.5 8.9 %collective-permute-start.2 = (f32[2,256,10,1]{1,0,3,2:T(2,128)S(1)}, f32[2,256,10,1]{1,0,3,2:T(2,128)S(1)}, u32[]{:S(2)}, u32[]{:S(2)}) collective-permute-start(f32[2,256,10,1]{1,0,3,2:T(2,128)S(1)} %get-tuple-element.40), channel_id=1, source_target_pairs={{0,8},{8,16},{16,24},{24,32},{32,40},{40,48},{48,56},{56,64},{64,7... | collective-permute-start | bytes 61448 | tf_op jit(solution)/shard_map/ppermute | solution.py:15
  81.6 8.8 %collective-permute-start.3 = (f32[2,256,10,1]{1,0,3,2:T(2,128)S(1)}, f32[2,256,10,1]{1,0,3,2:T(2,128)S(1)}, u32[]{:S(2)}, u32[]{:S(2)}) collective-permute-start(f32[2,256,10,1]{1,0,3,2:T(2,128)S(1)} %get-tuple-element.41), channel_id=1, source_target_pairs={{8,0},{16,8},{24,16},{32,24},{40,32},{48,40},{56,48},{64,56},{72,6... | collective-permute-start | bytes 61448 | tf_op jit(solution)/shard_map/ppermute | solution.py:16
  112.9 12.0 %copy-start.16 = (s32[1,1,256]{2,1,0:T(1,128)S(1)}, s32[1,1,256]{2,1,0:T(1,128)}, u32[]{:S(2)}) copy-start(s32[1,1,256]{2,1,0:T(1,128)} %param.8) | copy-start | bytes 3076
  113.6 29.0 %copy-start.2 = (f32[256,8,256]{0,2,1:T(8,128)}, f32[256,8,256]{0,2,1:T(8,128)S(1)}, u32[]{:S(2)}) copy-start(f32[256,8,256]{0,2,1:T(8,128)S(1)} %fusion.27) | copy-start | bytes 6291460
  113.6 22.0 %collective-permute-start.4 = (f32[1,256,1,256]{1,3,2,0:T(8,128)S(1)}, f32[1,256,1,256]{1,3,2,0:T(8,128)S(1)}, u32[]{:S(2)}, u32[]{:S(2)}) collective-permute-start(f32[1,256,1,256]{1,3,2,0:T(8,128)S(1)} %get-tuple-element.52), channel_id=1, source_target_pairs={{0,1},{1,2},{2,3},{3,4},{4,5},{5,6},{6,7},{8,9},{9,10},{10,11},{11... | collective-permute-start | bytes 786440 | tf_op jit(solution)/shard_map/ppermute | solution.py:15
  123.0 19.3 %collective-permute-start.5 = (f32[1,256,1,256]{1,3,2,0:T(8,128)S(1)}, f32[1,256,1,256]{1,3,2,0:T(8,128)S(1)}, u32[]{:S(2)}, u32[]{:S(2)}) collective-permute-start(f32[1,256,1,256]{1,3,2,0:T(8,128)S(1)} %get-tuple-element.53), channel_id=1, source_target_pairs={{1,0},{2,1},{3,2},{4,3},{5,4},{6,5},{7,6},{9,8},{10,9},{11,10},{12... | collective-permute-start | bytes 786440 | tf_op jit(solution)/shard_map/ppermute | solution.py:16
  144.1 12.4 %collective-permute-start.6 = (f32[1,256,10,1]{1,3,2,0:T(1,128)S(1)}, f32[1,256,10,1]{1,3,2,0:T(1,128)S(1)}, u32[]{:S(2)}, u32[]{:S(2)}) collective-permute-start(f32[1,256,10,1]{1,3,2,0:T(1,128)S(1)} %get-tuple-element.48), channel_id=1, source_target_pairs={{0,8},{8,16},{16,24},{24,32},{32,40},{40,48},{48,56},{56,64},{64,7... | collective-permute-start | bytes 30728 | tf_op jit(solution)/shard_map/ppermute | solution.py:15
  144.1 12.5 %collective-permute-start.7 = (f32[1,256,10,1]{1,3,2,0:T(1,128)S(1)}, f32[1,256,10,1]{1,3,2,0:T(1,128)S(1)}, u32[]{:S(2)}, u32[]{:S(2)}) collective-permute-start(f32[1,256,10,1]{1,3,2,0:T(1,128)S(1)} %get-tuple-element.49), channel_id=1, source_target_pairs={{8,0},{16,8},{24,16},{32,24},{40,32},{48,40},{56,48},{64,56},{72,6... | collective-permute-start | bytes 30728 | tf_op jit(solution)/shard_map/ppermute | solution.py:16
  150.0 9.3 %copy-start.18 = (f32[8]{0:T(128)}, f32[8]{0:T(128)S(1)}, u32[]{:S(2)}) copy-start(f32[8]{0:T(128)S(1)} %multiply_sine_fusion) | copy-start | bytes 100
  164.0 30.0 %copy-start.1 = (f32[1,256,8,256]{1,3,2,0:T(8,128)}, f32[1,256,8,256]{1,3,2,0:T(8,128)S(1)}, u32[]{:S(2)}) copy-start(f32[1,256,8,256]{1,3,2,0:T(8,128)S(1)} %get-tuple-element.27) | copy-start | bytes 6291460
  164.0 11.9 %copy-start.20 = (f32[1,1,256]{2,1,0:T(1,128)S(1)}, f32[1,1,256]{2,1,0:T(1,128)}, u32[]{:S(2)}) copy-start(f32[1,1,256]{2,1,0:T(1,128)} %param.11) | copy-start | bytes 3076
  164.1 29.9 %collective-permute-start.8 = (f32[2,256,1,256]{1,3,2,0:T(8,128)S(1)}, f32[2,256,1,256]{1,3,2,0:T(8,128)S(1)}, u32[]{:S(2)}, u32[]{:S(2)}) collective-permute-start(f32[2,256,1,256]{1,3,2,0:T(8,128)S(1)} %get-tuple-element.42), channel_id=1, source_target_pairs={{0,1},{1,2},{2,3},{3,4},{4,5},{5,6},{6,7},{8,9},{9,10},{10,11},{11... | collective-permute-start | bytes 1572872 | tf_op jit(solution)/shard_map/ppermute | solution.py:15
  170.5 23.5 %collective-permute-start.9 = (f32[2,256,1,256]{1,3,2,0:T(8,128)S(1)}, f32[2,256,1,256]{1,3,2,0:T(8,128)S(1)}, u32[]{:S(2)}, u32[]{:S(2)}) collective-permute-start(f32[2,256,1,256]{1,3,2,0:T(8,128)S(1)} %get-tuple-element.43), channel_id=1, source_target_pairs={{1,0},{2,1},{3,2},{4,3},{5,4},{6,5},{7,6},{9,8},{10,9},{11,10},{12... | collective-permute-start | bytes 1572872 | tf_op jit(solution)/shard_map/ppermute | solution.py:16
  194.0 21.6 %collective-permute-start.10 = (f32[2,256,10,1]{1,0,3,2:T(2,128)S(1)}, f32[2,256,10,1]{1,0,3,2:T(2,128)S(1)}, u32[]{:S(2)}, u32[]{:S(2)}) collective-permute-start(f32[2,256,10,1]{1,0,3,2:T(2,128)S(1)} %copy.49), channel_id=1, source_target_pairs={{0,8},{8,16},{16,24},{24,32},{32,40},{40,48},{48,56},{56,64},{64,7... | collective-permute-start | bytes 61448 | tf_op jit(solution)/shard_map/ppermute | solution.py:15
  194.2 21.5 %collective-permute-start.11 = (f32[2,256,10,1]{1,0,3,2:T(2,128)S(1)}, f32[2,256,10,1]{1,0,3,2:T(2,128)S(1)}, u32[]{:S(2)}, u32[]{:S(2)}) collective-permute-start(f32[2,256,10,1]{1,0,3,2:T(2,128)S(1)} %copy.50), channel_id=1, source_target_pairs={{8,0},{16,8},{24,16},{32,24},{40,32},{48,40},{56,48},{64,56},{72,6... | collective-permute-start | bytes 61448 | tf_op jit(solution)/shard_map/ppermute | solution.py:16
  223.9 298.5 %copy-start.22 = (s32[2]{0:T(128)S(1)}, s32[2]{0:T(128)}, u32[]{:S(2)}) copy-start(s32[2]{0:T(128)} %iota_multiply_fusion) | copy-start | bytes 28
  223.9 326.5 %collective-permute-start.12 = (f32[1,256,1,256]{1,3,2,0:T(8,128)}, f32[1,256,1,256]{1,3,2,0:T(8,128)S(1)}, u32[]{:S(2)}, u32[]{:S(2)}) collective-permute-start(f32[1,256,1,256]{1,3,2,0:T(8,128)} %get-tuple-element.50), channel_id=1, source_target_pairs={{0,1},{1,2},{2,3},{3,4},{4,5},{5,6},{6,7},{8,9},{9,10},{10,11},{11... | collective-permute-start | bytes 786440 | tf_op jit(solution)/shard_map/ppermute | solution.py:15
  231.2 319.2 %collective-permute-start.13 = (f32[1,256,1,256]{1,3,2,0:T(8,128)}, f32[1,256,1,256]{1,3,2,0:T(8,128)}, u32[]{:S(2)}, u32[]{:S(2)}) collective-permute-start(f32[1,256,1,256]{1,3,2,0:T(8,128)} %get-tuple-element.51), channel_id=1, source_target_pairs={{1,0},{2,1},{3,2},{4,3},{5,4},{6,5},{7,6},{9,8},{10,9},{11,10},{12... | collective-permute-start | bytes 786440 | tf_op jit(solution)/shard_map/ppermute | solution.py:16
  551.6 8.5 %collective-permute-start.14 = (f32[1,256,10,1]{1,3,2,0:T(1,128)S(1)}, f32[1,256,10,1]{1,3,2,0:T(1,128)S(1)}, u32[]{:S(2)}, u32[]{:S(2)}) collective-permute-start(f32[1,256,10,1]{1,3,2,0:T(1,128)S(1)} %get-tuple-element.46), channel_id=1, source_target_pairs={{0,8},{8,16},{16,24},{24,32},{32,40},{40,48},{48,56},{56,64},{64,7... | collective-permute-start | bytes 30728 | tf_op jit(solution)/shard_map/ppermute | solution.py:15
  551.6 8.4 %collective-permute-start.15 = (f32[1,256,10,1]{1,3,2,0:T(1,128)S(1)}, f32[1,256,10,1]{1,3,2,0:T(1,128)S(1)}, u32[]{:S(2)}, u32[]{:S(2)}) collective-permute-start(f32[1,256,10,1]{1,3,2,0:T(1,128)S(1)} %get-tuple-element.47), channel_id=1, source_target_pairs={{8,0},{16,8},{24,16},{32,24},{40,32},{48,40},{56,48},{64,56},{72,6... | collective-permute-start | bytes 30728 | tf_op jit(solution)/shard_map/ppermute | solution.py:16
  (16 other events, 30.3 us)
Sparse Core Ops, SparseCore 0:
  223.2 260.4 all-reduce.2
where the time goes:
time: 594 us; the launch traced here: 588 us
  waiting for transfers between devices  259 us (44%)
  other arithmetic  90 us (15%)
  blocking collectives  79 us (13%)
  starting transfers between devices  71.1 us (12%)
  local copies, waits for them, and re-layouts  61.1 us (10%)
  between operations  16.3 us (3%)
  matrix products  11.2 us (2%)
    psum x1, waiting for transfers between devices, shards(): gram, proj = lax.psum((gram, proj), ('lon', 'lat'))  167 us
    psum x1, blocking collectives, shards(): gram, proj = lax.psum((gram, proj), ('lon', 'lat'))  79 us
    ppermute x8, waiting for transfers between devices, with_halo(): before = lax.ppermute(last, axis, up)  54.6 us
    ppermute x8, starting transfers between devices, with_halo(): after = lax.ppermute(first, axis, down)  38.8 us
    ppermute x8, waiting for transfers between devices, with_halo(): after = lax.ppermute(first, axis, down)  37 us
    another operation x7, other arithmetic, shards(): lower = jnp.linalg.cholesky(gram + eye)  34.7 us
    ppermute x8, starting transfers between devices, with_halo(): before = lax.ppermute(last, axis, up)  32.3 us
    another operation x3, other arithmetic, shards(): inv_lower = jax.scipy.linalg.solve_triangular(lower, eye, lower=True)  21.2 us
  transfers between devices with their start and end apart: 17, of which 7 were waited for; matrix products, arithmetic and copies ran while one was open for 14% of the time, Pallas kernels for 0%

commit v1 on v0

--- a/solution.py
+++ b/solution.py
@@ -65,7 +65,7 @@
     innov = (obs_value.reshape(-1) - hmean) / sigma * valid
     gram = jnp.dot(anomal, anomal.T, precision=lax.Precision.HIGHEST)
     proj = jnp.dot(anomal, innov, precision=lax.Precision.HIGHEST)
-    gram, proj = lax.psum((gram, proj), ("lon", "lat"))
+    gram, proj = jax.lax.psum(jax.lax.psum((gram, proj), "lat"), "lon")
     eye = jnp.eye(members, dtype=jnp.float32)
     lower = jnp.linalg.cholesky(gram + eye)
     inv_lower = jax.scipy.linalg.solve_triangular(lower, eye, lower=True)

time: 594 us -> 728 us (1.23)
  waiting for transfers between devices: 259 us -> 366 us
  blocking collectives: 79 us -> 96.3 us
    psum x1 -> x2, waiting for transfers between devices: 167 us -> 261 us  [shards(): gram, proj = jax.lax.psum(jax.lax.psum((gram, proj), 'lat'), 'lon')]
    psum x1 -> x2, blocking collectives: 79 us -> 96.3 us  [shards(): gram, proj = jax.lax.psum(jax.lax.psum((gram, proj), 'lat'), 'lon')]
    ppermute x8, waiting for transfers between devices: 54.6 us -> 62.9 us  [with_halo(): before = lax.ppermute(last, axis, up)]
    unnamed x52 -> x58, local copies, waits for them, and re-layouts: 20.5 us -> 23.2 us
  transfers between devices with their start and end apart: 17 -> 18, of which waited for: 7 -> 9; matrix products, arithmetic and copies ran while one was open for 14% -> 4% of each run, Pallas kernels for 0% -> 0%
where the time goes in v1:
time: 728 us; the launch traced here: 721 us
  waiting for transfers between devices  366 us (50%)
  blocking collectives  96.3 us (13%)
  other arithmetic  91.4 us (13%)
  starting transfers between devices  71.3 us (10%)
  local copies, waits for them, and re-layouts  66.9 us (9%)
  between operations  16.4 us (2%)
  matrix products  12.7 us (2%)
    psum x2, waiting for transfers between devices, shards(): gram, proj = jax.lax.psum(jax.lax.psum((gram, proj), 'lat'), 'lon')  261 us
    psum x2, blocking collectives, shards(): gram, proj = jax.lax.psum(jax.lax.psum((gram, proj), 'lat'), 'lon')  96.3 us
    ppermute x8, waiting for transfers between devices, with_halo(): before = lax.ppermute(last, axis, up)  62.9 us
    ppermute x8, waiting for transfers between devices, with_halo(): after = lax.ppermute(first, axis, down)  41.4 us
    ppermute x8, starting transfers between devices, with_halo(): after = lax.ppermute(first, axis, down)  39.1 us
    another operation x7, other arithmetic, shards(): lower = jnp.linalg.cholesky(gram + eye)  34.8 us
    ppermute x8, starting transfers between devices, with_halo(): before = lax.ppermute(last, axis, up)  32.1 us
    unnamed x58, local copies, waits for them, and re-layouts  23.2 us
  transfers between devices with their start and end apart: 18, of which 9 were waited for; matrix products, arithmetic and copies ran while one was open for 4% of the time, Pallas kernels for 0%

profile of v1, /device:TPU:8, one launch (start us, length us, event | category | flops | bytes accessed | tf_op | source)
XLA Modules:
  0.0 720.6 jit_solution(6565714652809119836)
XLA Ops:
  27.3 9.1 %collective-permute-start = (f32[2,256,1,256]{1,0,3,2:T(2,128)S(1)}, f32[2,256,1,256]{1,0,3,2:T(2,128)S(1)}, u32[]{:S(2)}, u32[]{:S(2)}) collective-permute-start(f32[2,256,1,256]{1,0,3,2:T(2,128)S(1)} %get-tuple-element.44), channel_id=1, source_target_pairs={{0,1},{1,2},{2,3},{3,4},{4,5},{5,6},{6,7},{8,9},{9,10},{10,11},{11... | collective-permute-start | bytes 1572872 | tf_op jit(solution)/shard_map/ppermute | solution.py:15
  38.4 12.9 %collective-permute-done = f32[2,256,1,256]{1,0,3,2:T(2,128)S(1)} collective-permute-done((f32[2,256,1,256]{1,0,3,2:T(2,128)S(1)}, f32[2,256,1,256]{1,0,3,2:T(2,128)S(1)}, u32[]{:S(2)}, u32[]{:S(2)}) %collective-permute-start) | collective-permute-done | bytes 524320 | tf_op jit(solution)/shard_map/ppermute | solution.py:15
  51.3 30.3 %collective-permute-done.1 = f32[2,256,1,256]{1,0,3,2:T(2,128)S(1)} collective-permute-done((f32[2,256,1,256]{1,0,3,2:T(2,128)S(1)}, f32[2,256,1,256]{1,0,3,2:T(2,128)S(1)}, u32[]{:S(2)}, u32[]{:S(2)}) %collective-permute-start.1) | collective-permute-done | bytes 524320 | tf_op jit(solution)/shard_map/ppermute | solution.py:16
  81.7 6.2 collective-permute-start.3
  90.9 9.7 %pad_maximum_fusion.2 = f32[2,256,10,258]{1,0,3,2:T(2,128)} fusion(f32[2,256,10,1]{1,0,3,2:T(2,128)S(1)} %collective-permute-done.3, f32[2,256,1,256]{1,0,3,2:T(2,128)S(1)} %collective-permute-done.1, f32[1,256,8,256]{1,0,3,2:T(1,128)} %copy-done, f32[1,256,8,256]{1,0,3,2:T(1,128)S(1)} %copy.43, f32[2,256,1,256]{1,0,3,2:T(2,128)S(1)} %collective-permute-done, ...), kind=kLoop, calls=%fused_computation.8 | loop fusion | flops 6604800 | bytes 10567680 | tf_op jit(solution)/shard_map/concatenate | solution.py:17
  100.7 10.3 %fusion.63 = (f32[1,256,10,258]{1,0,3,2:T(1,128)S(1)}, f32[1,256,10,258]{1,0,3,2:T(1,128)}) fusion(f32[2,256,10,258]{1,0,3,2:T(2,128)} %pad_maximum_fusion.2), kind=kLoop, calls=%fused_computation.141 | loop fusion | bytes 10567680 | tf_op jit(solution)/shard_map/slice | solution.py:32
  114.1 9.3 %collective-permute-start.4 = (f32[1,256,1,256]{1,3,2,0:T(8,128)S(1)}, f32[1,256,1,256]{1,3,2,0:T(8,128)S(1)}, u32[]{:S(2)}, u32[]{:S(2)}) collective-permute-start(f32[1,256,1,256]{1,3,2,0:T(8,128)S(1)} %get-tuple-element.52), channel_id=1, source_target_pairs={{0,1},{1,2},{2,3},{3,4},{4,5},{5,6},{6,7},{8,9},{9,10},{10,11},{11... | collective-permute-start | bytes 786440 | tf_op jit(solution)/shard_map/ppermute | solution.py:15
  125.4 10.7 %collective-permute-done.4 = f32[1,256,1,256]{1,3,2,0:T(8,128)S(1)} collective-permute-done((f32[1,256,1,256]{1,3,2,0:T(8,128)S(1)}, f32[1,256,1,256]{1,3,2,0:T(8,128)S(1)}, u32[]{:S(2)}, u32[]{:S(2)}) %collective-permute-start.4) | collective-permute-done | bytes 262176 | tf_op jit(solution)/shard_map/ppermute | solution.py:15
  136.1 6.7 collective-permute-done.5
  164.5 6.3 collective-permute-start.8
  177.0 17.3 %collective-permute-done.8 = f32[2,256,1,256]{1,3,2,0:T(8,128)S(1)} collective-permute-done((f32[2,256,1,256]{1,3,2,0:T(8,128)S(1)}, f32[2,256,1,256]{1,3,2,0:T(8,128)S(1)}, u32[]{:S(2)}, u32[]{:S(2)}) %collective-permute-start.8) | collective-permute-done | bytes 524320 | tf_op jit(solution)/shard_map/ppermute | solution.py:15
  194.5 7.5 %collective-permute-start.11 = (f32[2,256,10,1]{1,0,3,2:T(2,128)S(1)}, f32[2,256,10,1]{1,0,3,2:T(2,128)S(1)}, u32[]{:S(2)}, u32[]{:S(2)}) collective-permute-start(f32[2,256,10,1]{1,0,3,2:T(2,128)S(1)} %copy.50), channel_id=1, source_target_pairs={{8,0},{16,8},{24,16},{32,24},{40,32},{48,40},{56,48},{64,56},{72,6... | collective-permute-start | bytes 61448 | tf_op jit(solution)/shard_map/ppermute | solution.py:16
  202.5 13.5 %collective-permute-done.10 = f32[2,256,10,1]{1,0,3,2:T(2,128)S(1)} collective-permute-done((f32[2,256,10,1]{1,0,3,2:T(2,128)S(1)}, f32[2,256,10,1]{1,0,3,2:T(2,128)S(1)}, u32[]{:S(2)}, u32[]{:S(2)}) %collective-permute-start.10) | collective-permute-done | bytes 20512 | tf_op jit(solution)/shard_map/ppermute | solution.py:15
  221.3 7.2 collective-permute-start.12
  237.2 8.4 %collective-permute-done.12 = f32[1,256,1,256]{1,3,2,0:T(8,128)S(1)} collective-permute-done((f32[1,256,1,256]{1,3,2,0:T(8,128)}, f32[1,256,1,256]{1,3,2,0:T(8,128)S(1)}, u32[]{:S(2)}, u32[]{:S(2)}) %collective-permute-start.12) | collective-permute-done | bytes 262176 | tf_op jit(solution)/shard_map/ppermute | solution.py:15
  257.8 27.8 %psum.30 = f32[256]{0:T(256)S(1)} all-reduce(f32[256]{0:T(256)S(1)} %bitcast.156), channel_id=1, replica_groups=mesh['lon'=32,'lat'=8] {'lat'}, use_global_device_ids=true, to_apply=%region_8.9 | all-reduce | flops 256 | bytes 2048 | tf_op jit(solution)/shard_map/psum | solution.py:68
  285.6 68.6 %psum.31 = f32[256]{0:T(256)S(1)} all-reduce(f32[256]{0:T(256)S(1)} %psum.30), channel_id=1, replica_groups=mesh['lon'=32,'lat'=8] {'lon'}, use_global_device_ids=true, to_apply=%region_9.10 | all-reduce | flops 256 | bytes 2048 | tf_op jit(solution)/shard_map/psum | solution.py:68
  370.3 261.3 %all-reduce.6.cloned.1.call-done = f32[256,256]{0,1:T(8,128)} async-done(((f32[256,256]{0,1:T(8,128)}), f32[256,256]{0,1:T(8,128)}) %all-reduce.6.cloned.1.call-update) | async-done | bytes 262160 | tf_op jit(solution)/shard_map/psum | solution.py:68
  633.7 11.7 %cholesky.49 = f32[128,128]{1,0:T(8,128)S(1)} custom-call(f32[128,128]{1,0:T(8,128)S(1)} %cholesky.115), custom_call_target="Cholesky" | custom-call | tf_op jit(solution)/shard_map/jit(cholesky)/cholesky | solution.py:70
  645.5 9.8 %custom-call.21 = f32[1,128,128]{1,2,0:T(8,128)S(1)} custom-call(f32[1,128,128]{2,1,0:T(8,128)S(1)} %get-tuple-element.57), custom_call_target="InvertDiagBlocksLowerTriangular" | custom-call | tf_op jit(solution)/shard_map/jit(cholesky)/cholesky | solution.py:70
  655.8 11.9 %cholesky.103 = f32[128,128]{1,0:T(8,128)S(1)} custom-call(f32[128,128]{1,0:T(8,128)S(1)} %convolution_subtract_fusion.1), custom_call_target="Cholesky" | custom-call | tf_op jit(solution)/shard_map/jit(cholesky)/cholesky | solution.py:70
  675.5 20.5 %custom-call.22 = f32[2,128,128]{1,2,0:T(8,128)S(1)} custom-call(f32[2,128,128]{2,1,0:T(8,128)} %get-tuple-element.12), custom_call_target="InvertDiagBlocksLowerTriangular" | custom-call | tf_op jit(solution)/shard_map/jit(_solve_triangular)/triangular_solve | solution.py:71
  698.1 8.5 %add_bitcast_fusion = f32[3,256,8,256]{1,3,2,0:T(8,128)} fusion(f32[3,8,256]{2,1,0:T(8,128)S(1)} %broadcast_multiply_fusion.2, f32[1,256,8,256]{1,3,2,0:T(8,128)} %copy-done.5, f32[1,256,8,256]{1,3,2,0:T(8,128)} %copy-done.4, f32[1,256,8,256]{1,3,2,0:T(8,128)S(1)} %bitcast.145, f32[128,256]{1,0:T(8,128)S(1)} %fusion.48, f32[128,256]{1,0:T(8,128)S(1)} %fusion.40, ...), kind=kOutput, calls=%fused_computation.4 | convolution fusion | flops 4838260736 | bytes 12870656 | tf_op jit(solution)/shard_map/nm,cnab->cmab/dot_general | solution.py:76
  706.7 6.6 copy.59
  (158 shorter events, 117.1 us)
Async XLA Ops:
  6.5 353.5 %all-reduce.4.cloned.1.call-start = ((), (), s32[]{:S(2)}) async-start(), calls=%async_computation | async-start | bytes 524288 | tf_op jit(solution)/shard_map/psum | solution.py:68
  26.4 55.2 %copy-start = (f32[1,256,8,256]{1,0,3,2:T(1,128)}, f32[1,256,8,256]{1,0,3,2:T(1,128)S(1)}, u32[]{:S(2)}) copy-start(f32[1,256,8,256]{1,0,3,2:T(1,128)S(1)} %broadcast_multiply_fusion) | copy-start | bytes 6291460
  27.3 24.0 %collective-permute-start = (f32[2,256,1,256]{1,0,3,2:T(2,128)S(1)}, f32[2,256,1,256]{1,0,3,2:T(2,128)S(1)}, u32[]{:S(2)}, u32[]{:S(2)}) collective-permute-start(f32[2,256,1,256]{1,0,3,2:T(2,128)S(1)} %get-tuple-element.44), channel_id=1, source_target_pairs={{0,1},{1,2},{2,3},{3,4},{4,5},{5,6},{6,7},{8,9},{9,10},{10,11},{11... | collective-permute-start | bytes 1572872 | tf_op jit(solution)/shard_map/ppermute | solution.py:15
  36.5 45.1 %collective-permute-start.1 = (f32[2,256,1,256]{1,0,3,2:T(2,128)S(1)}, f32[2,256,1,256]{1,0,3,2:T(2,128)S(1)}, u32[]{:S(2)}, u32[]{:S(2)}) collective-permute-start(f32[2,256,1,256]{1,0,3,2:T(2,128)S(1)} %get-tuple-element.45), channel_id=1, source_target_pairs={{1,0},{2,1},{3,2},{4,3},{5,4},{6,5},{7,6},{9,8},{10,9},{11,10},{12... | collective-permute-start | bytes 1572872 | tf_op jit(solution)/shard_map/ppermute | solution.py:16
  81.6 9.3 %collective-permute-start.2 = (f32[2,256,10,1]{1,0,3,2:T(2,128)S(1)}, f32[2,256,10,1]{1,0,3,2:T(2,128)S(1)}, u32[]{:S(2)}, u32[]{:S(2)}) collective-permute-start(f32[2,256,10,1]{1,0,3,2:T(2,128)S(1)} %get-tuple-element.40), channel_id=1, source_target_pairs={{0,8},{8,16},{16,24},{24,32},{32,40},{40,48},{48,56},{56,64},{64,7... | collective-permute-start | bytes 61448 | tf_op jit(solution)/shard_map/ppermute | solution.py:15
  81.7 9.2 %collective-permute-start.3 = (f32[2,256,10,1]{1,0,3,2:T(2,128)S(1)}, f32[2,256,10,1]{1,0,3,2:T(2,128)S(1)}, u32[]{:S(2)}, u32[]{:S(2)}) collective-permute-start(f32[2,256,10,1]{1,0,3,2:T(2,128)S(1)} %get-tuple-element.41), channel_id=1, source_target_pairs={{8,0},{16,8},{24,16},{32,24},{40,32},{48,40},{56,48},{64,56},{72,6... | collective-permute-start | bytes 61448 | tf_op jit(solution)/shard_map/ppermute | solution.py:16
  114.1 29.0 %copy-start.2 = (f32[256,8,256]{0,2,1:T(8,128)}, f32[256,8,256]{0,2,1:T(8,128)S(1)}, u32[]{:S(2)}) copy-start(f32[256,8,256]{0,2,1:T(8,128)S(1)} %fusion.27) | copy-start | bytes 6291460
  114.1 22.0 %collective-permute-start.4 = (f32[1,256,1,256]{1,3,2,0:T(8,128)S(1)}, f32[1,256,1,256]{1,3,2,0:T(8,128)S(1)}, u32[]{:S(2)}, u32[]{:S(2)}) collective-permute-start(f32[1,256,1,256]{1,3,2,0:T(8,128)S(1)} %get-tuple-element.52), channel_id=1, source_target_pairs={{0,1},{1,2},{2,3},{3,4},{4,5},{5,6},{6,7},{8,9},{9,10},{10,11},{11... | collective-permute-start | bytes 786440 | tf_op jit(solution)/shard_map/ppermute | solution.py:15
  123.4 19.4 %collective-permute-start.5 = (f32[1,256,1,256]{1,3,2,0:T(8,128)S(1)}, f32[1,256,1,256]{1,3,2,0:T(8,128)S(1)}, u32[]{:S(2)}, u32[]{:S(2)}) collective-permute-start(f32[1,256,1,256]{1,3,2,0:T(8,128)S(1)} %get-tuple-element.53), channel_id=1, source_target_pairs={{1,0},{2,1},{3,2},{4,3},{5,4},{6,5},{7,6},{9,8},{10,9},{11,10},{12... | collective-permute-start | bytes 786440 | tf_op jit(solution)/shard_map/ppermute | solution.py:16
  144.6 12.4 %collective-permute-start.6 = (f32[1,256,10,1]{1,3,2,0:T(1,128)S(1)}, f32[1,256,10,1]{1,3,2,0:T(1,128)S(1)}, u32[]{:S(2)}, u32[]{:S(2)}) collective-permute-start(f32[1,256,10,1]{1,3,2,0:T(1,128)S(1)} %get-tuple-element.48), channel_id=1, source_target_pairs={{0,8},{8,16},{16,24},{24,32},{32,40},{40,48},{48,56},{56,64},{64,7... | collective-permute-start | bytes 30728 | tf_op jit(solution)/shard_map/ppermute | solution.py:15
  144.6 12.4 %collective-permute-start.7 = (f32[1,256,10,1]{1,3,2,0:T(1,128)S(1)}, f32[1,256,10,1]{1,3,2,0:T(1,128)S(1)}, u32[]{:S(2)}, u32[]{:S(2)}) collective-permute-start(f32[1,256,10,1]{1,3,2,0:T(1,128)S(1)} %get-tuple-element.49), channel_id=1, source_target_pairs={{8,0},{16,8},{24,16},{32,24},{40,32},{48,40},{56,48},{64,56},{72,6... | collective-permute-start | bytes 30728 | tf_op jit(solution)/shard_map/ppermute | solution.py:16
  164.4 29.9 %copy-start.1 = (f32[1,256,8,256]{1,3,2,0:T(8,128)}, f32[1,256,8,256]{1,3,2,0:T(8,128)S(1)}, u32[]{:S(2)}) copy-start(f32[1,256,8,256]{1,3,2,0:T(8,128)S(1)} %get-tuple-element.27) | copy-start | bytes 6291460
  164.5 29.8 %collective-permute-start.8 = (f32[2,256,1,256]{1,3,2,0:T(8,128)S(1)}, f32[2,256,1,256]{1,3,2,0:T(8,128)S(1)}, u32[]{:S(2)}, u32[]{:S(2)}) collective-permute-start(f32[2,256,1,256]{1,3,2,0:T(8,128)S(1)} %get-tuple-element.42), channel_id=1, source_target_pairs={{0,1},{1,2},{2,3},{3,4},{4,5},{5,6},{6,7},{8,9},{9,10},{10,11},{11... | collective-permute-start | bytes 1572872 | tf_op jit(solution)/shard_map/ppermute | solution.py:15
  170.8 23.5 %collective-permute-start.9 = (f32[2,256,1,256]{1,3,2,0:T(8,128)S(1)}, f32[2,256,1,256]{1,3,2,0:T(8,128)S(1)}, u32[]{:S(2)}, u32[]{:S(2)}) collective-permute-start(f32[2,256,1,256]{1,3,2,0:T(8,128)S(1)} %get-tuple-element.43), channel_id=1, source_target_pairs={{1,0},{2,1},{3,2},{4,3},{5,4},{6,5},{7,6},{9,8},{10,9},{11,10},{12... | collective-permute-start | bytes 1572872 | tf_op jit(solution)/shard_map/ppermute | solution.py:16
  194.4 21.6 %collective-permute-start.10 = (f32[2,256,10,1]{1,0,3,2:T(2,128)S(1)}, f32[2,256,10,1]{1,0,3,2:T(2,128)S(1)}, u32[]{:S(2)}, u32[]{:S(2)}) collective-permute-start(f32[2,256,10,1]{1,0,3,2:T(2,128)S(1)} %copy.49), channel_id=1, source_target_pairs={{0,8},{8,16},{16,24},{24,32},{32,40},{40,48},{48,56},{56,64},{64,7... | collective-permute-start | bytes 61448 | tf_op jit(solution)/shard_map/ppermute | solution.py:15
  194.5 21.5 %collective-permute-start.11 = (f32[2,256,10,1]{1,0,3,2:T(2,128)S(1)}, f32[2,256,10,1]{1,0,3,2:T(2,128)S(1)}, u32[]{:S(2)}, u32[]{:S(2)}) collective-permute-start(f32[2,256,10,1]{1,0,3,2:T(2,128)S(1)} %copy.50), channel_id=1, source_target_pairs={{8,0},{16,8},{24,16},{32,24},{40,32},{48,40},{56,48},{64,56},{72,6... | collective-permute-start | bytes 61448 | tf_op jit(solution)/shard_map/ppermute | solution.py:16
  220.5 15.1 %copy-start.17 = (f32[256]{0:T(256)S(1)}, f32[256]{0:T(256)}, u32[]{:S(2)}) copy-start(f32[256]{0:T(256)} %get-tuple-element.67) | copy-start | bytes 3076
  220.5 15.1 %copy-start.18 = (f32[1,1,256]{2,1,0:T(1,128)S(1)}, f32[1,1,256]{2,1,0:T(1,128)}, u32[]{:S(2)}) copy-start(f32[1,1,256]{2,1,0:T(1,128)} %get-tuple-element.61) | copy-start | bytes 3076
  221.3 24.3 %collective-permute-start.12 = (f32[1,256,1,256]{1,3,2,0:T(8,128)}, f32[1,256,1,256]{1,3,2,0:T(8,128)S(1)}, u32[]{:S(2)}, u32[]{:S(2)}) collective-permute-start(f32[1,256,1,256]{1,3,2,0:T(8,128)} %get-tuple-element.50), channel_id=1, source_target_pairs={{0,1},{1,2},{2,3},{3,4},{4,5},{5,6},{6,7},{8,9},{9,10},{10,11},{11... | collective-permute-start | bytes 786440 | tf_op jit(solution)/shard_map/ppermute | solution.py:15
  228.5 21.5 %collective-permute-start.13 = (f32[1,256,1,256]{1,3,2,0:T(8,128)}, f32[1,256,1,256]{1,3,2,0:T(8,128)S(1)}, u32[]{:S(2)}, u32[]{:S(2)}) collective-permute-start(f32[1,256,1,256]{1,3,2,0:T(8,128)} %get-tuple-element.51), channel_id=1, source_target_pairs={{1,0},{2,1},{3,2},{4,3},{5,4},{6,5},{7,6},{9,8},{10,9},{11,10},{12... | collective-permute-start | bytes 786440 | tf_op jit(solution)/shard_map/ppermute | solution.py:16
  237.2 394.4 %all-reduce.6.cloned.1.call-start = ((), (), s32[]{:S(2)}) async-start(), calls=%async_computation.1 | async-start | bytes 524288 | tf_op jit(solution)/shard_map/psum | solution.py:68
  251.9 108.2 %collective-permute-start.14 = (f32[1,256,10,1]{1,3,2,0:T(1,128)S(1)}, f32[1,256,10,1]{1,3,2,0:T(1,128)S(1)}, u32[]{:S(2)}, u32[]{:S(2)}) collective-permute-start(f32[1,256,10,1]{1,3,2,0:T(1,128)S(1)} %get-tuple-element.46), channel_id=1, source_target_pairs={{0,8},{8,16},{16,24},{24,32},{32,40},{40,48},{48,56},{56,64},{64,7... | collective-permute-start | bytes 30728 | tf_op jit(solution)/shard_map/ppermute | solution.py:15
  252.0 108.2 %collective-permute-start.15 = (f32[1,256,10,1]{1,3,2,0:T(1,128)S(1)}, f32[1,256,10,1]{1,3,2,0:T(1,128)S(1)}, u32[]{:S(2)}, u32[]{:S(2)}) collective-permute-start(f32[1,256,10,1]{1,3,2,0:T(1,128)S(1)} %get-tuple-element.47), channel_id=1, source_target_pairs={{8,0},{16,8},{24,16},{32,24},{40,32},{48,40},{56,48},{64,56},{72,6... | collective-permute-start | bytes 30728 | tf_op jit(solution)/shard_map/ppermute | solution.py:16
  370.3 300.0 %copy-start.25 = (s32[2]{0:T(128)S(1)}, s32[2]{0:T(128)}, u32[]{:S(2)}) copy-start(s32[2]{0:T(128)} %iota_multiply_fusion) | copy-start | bytes 28
  (20 other events, 107.0 us)
Sparse Core Ops, SparseCore 0:
  237.3 106.8 all-reduce.3
  360.2 271.3 all-reduce.5
